TPU v7x, 512 devices: a whole 4x8x8 slice. The times are simulated.
512 devices in a mesh: row: 16 (over z, y_lo), col: 8 (over y_hi, core), rep: 4 (over x).
Axes of the slice: x: 4, y: 8 (y_hi: 4, y_lo: 2; y = y_hi * 2 + y_lo), z: 8, core: 2. Of those that a mesh axis runs over, the one named last changes fastest.
Arguments:
- genotypes: bfloat16 [2048, 16384], P(('row', 'col', 'rep')), may hold values from 0 to 2, as said below
Outputs:
- main_tiles: float32 [16, 8, 1024, 1024], P('row', 'col', 'rep')
- half_tiles: float32 [16, 1024, 1024], P('row', 'rep', 'col')
Inputs may be any that keep to these rules, and one draw needn't show every extreme that they name: `genotypes`: imputed dosages of the alternate allele, real-valued.
All inputs are finite; a program needn't handle non-finite values.
Results may differ from a plain program's by a relative error of at most 0.008.
Values may be sent and summed in bfloat16 or wider, within the bound.
No kernel may reach another device: no remote copies, remote signals or barrier semaphores. Data moves between devices by JAX's collectives and lax.ppermute only.
A program may use at most 64 MiB of HBM per device.

v0:
```python
import jax
import jax.numpy as jnp
import numpy as np
from jax import lax
from jax.sharding import PartitionSpec as P


def copy_for_each(x, axis):
    copies = jnp.broadcast_to(x, (lax.axis_size(axis), *x.shape))
    return lax.all_to_all(copies, axis, split_axis=0, concat_axis=0, tiled=True)


def over_copies(x, axis):
    return copy_for_each(x, axis).sum(axis=0)


def packed_total(arrays, axis):
    ends = [0]
    for a in arrays:
        ends.append(ends[-1] + a.size)
    total = over_copies(jnp.concatenate([a.ravel() for a in arrays]), axis)
    return tuple((total[b:e].reshape(a.shape) for a, b, e in zip(arrays, ends, ends[1:])))


def cut_along(x, dim, length):
    before, after = (x.shape[:dim], x.shape[dim + 1 :])
    return jnp.moveaxis(x.reshape(*before, length, -1, *after), dim, 0)


def summed_on_arrival(x, axis, dim):
    length = lax.axis_size(axis)
    blocks = lax.all_to_all(cut_along(x, dim, length), axis, 0, 0, tiled=True)
    return jnp.sum(blocks.astype(jnp.float32), axis=0)


def body(genotypes):
    sample_rows, variants = genotypes.shape
    row_count = lax.axis_size("row")
    col_count = lax.axis_size("col")
    rep_count = lax.axis_size("rep")
    sample_count = sample_rows * row_count * col_count * rep_count
    block_width = variants // row_count
    slab_width = block_width // col_count
    pair_count = row_count * col_count
    blocked = genotypes.reshape(sample_rows, row_count, block_width)
    shift_table = np.array(
        [(brow + bcol) % row_count for brow in range(row_count) for bcol in range(col_count)],
        np.int32,
    )
    partner = jnp.take(blocked, shift_table, axis=1)
    slab_view = genotypes.reshape(sample_rows, pair_count, slab_width)
    far_slab = jnp.roll(slab_view, -(pair_count // 2), axis=1)
    own_block = jnp.broadcast_to(
        blocked[:, :, None, :], (sample_rows, row_count, col_count, block_width)
    )
    payload = jnp.concatenate(
        [partner, own_block.reshape(sample_rows, pair_count, block_width), far_slab], axis=2
    )
    payload_width = payload.shape[2]
    arrived = lax.all_to_all(payload, ("row", "col"), split_axis=1, concat_axis=0, tiled=True)
    arrived = arrived.reshape(-1, payload_width)
    values = arrived.astype(jnp.float32)
    col_dose, col_square = packed_total(
        (jnp.sum(values, axis=0), jnp.sum(values * values, axis=0)), "rep"
    )
    col_mean = col_dose / sample_count
    col_spread = col_square / sample_count - col_mean * col_mean
    arrived = ((values - col_mean) * lax.rsqrt(col_spread + 1e-05)).astype(jnp.bfloat16)
    scale_factor = 1.0 / sample_count
    right_side = jnp.concatenate(
        [arrived[:, :block_width], arrived[:, payload_width - slab_width :]], axis=1
    )
    product = lax.dot_general(
        arrived[:, block_width : 2 * block_width],
        right_side,
        (((0,), (0,)), ((), ())),
        preferred_element_type=jnp.float32,
    )
    partial_value = product * scale_factor
    summed = summed_on_arrival(partial_value.astype(jnp.bfloat16), "rep", 0)
    main_tile = summed[:, :block_width].reshape(1, 1, -1, block_width)
    half_tile = summed[:, block_width:].reshape(1, -1, slab_width)
    return (main_tile, half_tile)


def solution(mesh):
    placed = (P(("row", "col", "rep"), None),)
    return jax.shard_map(
        body,
        mesh=mesh,
        in_specs=placed,
        out_specs=(P("row", "col", "rep", None), P("row", "rep", "col")),
        check_vma=False,
    )
```

profile of v0, /device:TPU:9, one launch (start us, length us, event | category | flops | bytes accessed | tf_op | source)
XLA Modules:
  0.0 138.4 jit_solution(16736934565368421999)
XLA Ops:
  0.6 0.0 copy-start
  0.6 0.7 pad_clamp_fusion
  1.3 0.9 fusion.10
  2.3 2.4 %gather_fusion = bf16[128,4,1024]{2,1,0:T(4,128)(2,1)S(1)} fusion(bf16[4,16,1024]{2,0,1:T(4,128)(2,1)} %bitcast.16, s32[1024]{0:T(1024)S(1)} %pad_clamp_fusion), kind=kCustom, calls=%fused_computation | custom fusion | bytes 2097664 | tf_op jit(solution)/shard_map/jit(_take)/gather | solution.py:50
  4.6 0.0 copy-done
  4.6 0.3 broadcast_in_dim.25
  4.9 5.4 %maximum_maximum_fusion = bf16[4,128,2176]{2,0,1:T(4,128)(2,1)S(1)} fusion(bf16[4,64,128]{2,0,1:T(4,128)(2,1)S(1)} %get-tuple-element.5, bf16[4,64,128]{2,0,1:T(4,128)(2,1)S(1)} %get-tuple-element.4, bf16[4,128,1024]{2,0,1:T(4,128)(2,1)S(1)} %bitcast.19, bf16[4,128,1024]{2,0,1:T(4,128)(2,1)S(1)} %bitcast.18), kind=kLoop, calls=%fused_computation.9 | loop fusion | flops 8912896 | bytes 4456448 | tf_op jit(solution)/shard_map/concatenate | solution.py:56
  10.4 73.1 %all_to_all.20 = bf16[4,128,2176]{2,0,1:T(4,128)(2,1)S(1)} all-to-all(bf16[4,128,2176]{2,0,1:T(4,128)(2,1)S(1)} %maximum_maximum_fusion), channel_id=1, replica_groups=mesh['row'=16,'col'=8,'rep'=4] {'row','col'}, dimensions={1} | all-to-all | bytes 4456448 | tf_op jit(solution)/shard_map/all_to_all | solution.py:60
  83.5 1.8 %convert_reduce_fusion = (f32[2176]{0:T(1024)S(1)}, f32[2176]{0:T(1024)S(1)}) fusion(bf16[4,128,2176]{2,0,1:T(4,128)(2,1)S(1)} %all_to_all.20), kind=kLoop, calls=%fused_computation.2 | loop fusion | flops 4452096 | bytes 2245632 | tf_op jit(solution)/shard_map/reduce_sum | solution.py:64
  85.3 0.7 broadcast_in_dim.26
  85.9 4.0 %all-to-all-start.1 = ((f32[4,1,4352]{2,1,0:T(1,128)}), f32[4,1,4352]{2,1,0:T(1,128)S(1)}, u32[]{:S(2)}, u32[]{:S(2)}) async-start(f32[4,1,4352]{2,1,0:T(1,128)} %broadcast_in_dim.26), calls=%async_computation.1 | async-start | bytes 139264 | tf_op jit(solution)/shard_map/all_to_all | solution.py:10
  89.9 2.6 %convert_bitcast_fusion = f32[128,4,1,2176]{3,1,0,2:T(4,128)} fusion(bf16[4,128,2176]{2,0,1:T(4,128)(2,1)S(1)} %all_to_all.20), kind=kLoop, calls=%fused_computation.3 | loop fusion | flops 1114112 | bytes 6684672 | tf_op jit(solution)/shard_map/convert_element_type | solution.py:62
  92.5 5.6 %reshape.48 = f32[512,2176]{1,0:T(8,128)} reshape(f32[128,4,1,2176]{3,1,0,2:T(4,128)} %convert_bitcast_fusion) | data formatting | bytes 8912896 | tf_op jit(solution)/shard_map/convert_element_type | solution.py:62
  98.1 0.0 all-to-all-done.1
  98.1 0.1 reduce_sum.38
  98.2 2.7 %multiply_convert_fusion = bf16[512,2176]{1,0:T(8,128)(2,1)S(1)} fusion(f32[512,2176]{1,0:T(8,128)} %reshape.48, f32[2176]{0:T(1024)S(1)} %get-tuple-element.7, f32[2176]{0:T(1024)S(1)} %get-tuple-element.6), kind=kLoop, calls=%fused_computation.7 | loop fusion | flops 3342336 | bytes 6702080 | tf_op jit(solution)/shard_map/convert_element_type | solution.py:68
  100.9 0.1 slice.45
  101.0 1.6 %fusion.1 = bf16[1024,1152]{1,0:T(8,128)(2,1)S(1)} fusion(bf16[512,128]{1,0:T(8,128)(2,1)S(1)} %slice.46, bf16[512,1024]{1,0:T(8,128)(2,1)S(1)} %slice.45, bf16[512,2176]{1,0:T(8,128)(2,1)S(1)} %multiply_convert_fusion), kind=kOutput, calls=%fused_computation.8 | convolution fusion | flops 1212678144 | bytes 4587520 | tf_op jit(solution)/shard_map/dot_general | solution.py:73
  102.6 33.7 %all_to_all.21 = bf16[4,256,1152]{2,1,0:T(8,128)(2,1)S(1)} all-to-all(bf16[4,256,1152]{2,1,0:T(8,128)(2,1)S(1)} %bitcast.20), channel_id=1, replica_groups=mesh['row'=16,'col'=8,'rep'=4] {'rep'}, dimensions={0} | all-to-all | bytes 4718592 | tf_op jit(solution)/shard_map/all_to_all | solution.py:32
  136.3 0.3 convert_reduce_fusion.1
  136.6 0.7 slice_bitcast_fusion.1
  137.3 1.1 slice_bitcast_fusion
  (3 shorter events, 0.0 us)
Async XLA Ops:
  0.6 4.0 %copy-start = (bf16[4,16384]{1,0:T(4,128)(2,1)S(1)}, bf16[4,16384]{1,0:T(4,128)(2,1)}, u32[]{:S(2)}) copy-start(bf16[4,16384]{1,0:T(4,128)(2,1)} %param.2) | copy-start | bytes 393220
  85.9 12.2 %all-to-all-start.1 = ((f32[4,1,4352]{2,1,0:T(1,128)}), f32[4,1,4352]{2,1,0:T(1,128)S(1)}, u32[]{:S(2)}, u32[]{:S(2)}) async-start(f32[4,1,4352]{2,1,0:T(1,128)} %broadcast_in_dim.26), calls=%async_computation.1 | async-start | bytes 139264 | tf_op jit(solution)/shard_map/all_to_all | solution.py:10
where the time goes:
time: 139 us; the launch traced here: 138 us
  blocking collectives  107 us (77%)
  other arithmetic  13.6 us (10%)
  local copies, waits for them, and re-layouts  11.7 us (8%)
  starting transfers between devices  4.01 us (3%)
  matrix products  1.59 us (1%)
    all_to_all x1, blocking collectives, body(): lax.all_to_all(payload, ('row', 'col'), split_axis=1, concat_axis=0, tile...  73.1 us
    all_to_all x1, blocking collectives, summed_on_arrival(): blocks = lax.all_to_all(cut_along(x, dim, length), axis, 0, 0, tiled=True)  33.7 us
    convert_element_type x1, local copies, waits for them, and re-layouts, body(): values = arrived.astype(jnp.float32)  5.55 us
    concatenate x1, other arithmetic, body(): jnp.concatenate([partner, own_block.reshape(sample_rows, pair_count, bloc...  5.44 us
    all_to_all x1, starting transfers between devices, copy_for_each(): return lax.all_to_all(copies, axis, split_axis=0, concat_axis=0, tiled=True)  4.01 us
  transfers between devices with their start and end apart: 1, of which 0 were waited for; matrix products, arithmetic and copies ran while one was open for 6% of the time, Pallas kernels for 0%

commit v1 on v0

--- a/solution.py
+++ b/solution.py
@@ -57,7 +57,9 @@
         [partner, own_block.reshape(sample_rows, pair_count, block_width), far_slab], axis=2
     )
     payload_width = payload.shape[2]
-    arrived = lax.all_to_all(payload, ("row", "col"), split_axis=1, concat_axis=0, tiled=True)
+    parts = jnp.split(payload, lax.axis_size(("row", "col")), axis=1)
+    got = lax.all_to_all(jnp.stack(parts), ("row", "col"), 0, 0)
+    arrived = jnp.concatenate(got, axis=0)
     arrived = arrived.reshape(-1, payload_width)
     values = arrived.astype(jnp.float32)
     col_dose, col_square = packed_total(

time: 139 us -> 136 us (0.978)
  other arithmetic: 13.6 us -> 11 us
  blocking collectives: 107 us -> 105 us
  waiting for transfers between devices: 0.01 us -> 1.94 us
    convert_element_type x1, local copies, waits for them, and re-layouts: 5.55 us -> 2.55 us  [body(): values = arrived.astype(jnp.float32)]
    convert_element_type x1 -> x0, other arithmetic: 2.61 us -> none  [body(): values = arrived.astype(jnp.float32)]
    all_to_all x1, blocking collectives: 33.7 us -> 31.5 us  [summed_on_arrival(): blocks = lax.all_to_all(cut_along(x, dim, length), axis, 0, 0, tiled=True)]
    unnamed x2 -> x129, local copies, waits for them, and re-layouts: 0.01 us -> 2.14 us
    all_to_all x1, waiting for transfers between devices: 0.01 us -> 1.94 us  [copy_for_each(): return lax.all_to_all(copies, axis, split_axis=0, concat_axis=0, tiled=True)]
  transfers between devices with their start and end apart: 1 -> 1, of which waited for: 0 -> 1; matrix products, arithmetic and copies ran while one was open for 6% -> 2% of each run, Pallas kernels for 0% -> 0%
where the time goes in v1:
time: 136 us; the launch traced here: 135 us
  blocking collectives  105 us (77%)
  other arithmetic  11 us (8%)
  local copies, waits for them, and re-layouts  10.9 us (8%)
  starting transfers between devices  4.01 us (3%)
  waiting for transfers between devices  1.94 us (1%)
  matrix products  1.59 us (1%)
    all_to_all x1, blocking collectives, body(): got = lax.all_to_all(jnp.stack(parts), ('row', 'col'), 0, 0)  73.1 us
    all_to_all x1, blocking collectives, summed_on_arrival(): blocks = lax.all_to_all(cut_along(x, dim, length), axis, 0, 0, tiled=True)  31.5 us
    concatenate x1, other arithmetic, body(): jnp.concatenate([partner, own_block.reshape(sample_rows, pair_count, bloc...  5.44 us
    all_to_all x1, starting transfers between devices, copy_for_each(): return lax.all_to_all(copies, axis, split_axis=0, concat_axis=0, tiled=True)  4.01 us
  transfers between devices with their start and end apart: 1, of which 1 were waited for; matrix products, arithmetic and copies ran while one was open for 2% of the time, Pallas kernels for 0%

profile of v1, /device:TPU:9, one launch (start us, length us, event | category | flops | bytes accessed | tf_op | source)
XLA Modules:
  0.0 135.3 jit_solution(6326807295650649874)
XLA Ops:
  0.6 0.0 copy-start
  0.6 0.7 pad_clamp_fusion
  1.3 0.9 fusion.9
  2.3 2.4 %gather_fusion = bf16[128,4,1024]{2,1,0:T(4,128)(2,1)S(1)} fusion(bf16[4,16,1024]{2,0,1:T(4,128)(2,1)} %bitcast.524, s32[1024]{0:T(1024)S(1)} %pad_clamp_fusion), kind=kCustom, calls=%fused_computation | custom fusion | bytes 2097664 | tf_op jit(solution)/shard_map/jit(_take)/gather | solution.py:50
  4.6 0.0 copy-done
  4.6 0.3 broadcast_in_dim.25
  4.9 5.4 %maximum_maximum_fusion = bf16[4,128,2176]{2,0,1:T(4,128)(2,1)S(1)} fusion(bf16[4,64,128]{2,0,1:T(4,128)(2,1)S(1)} %get-tuple-element.5, bf16[4,64,128]{2,0,1:T(4,128)(2,1)S(1)} %get-tuple-element.4, bf16[4,128,1024]{2,0,1:T(4,128)(2,1)S(1)} %bitcast.527, bf16[4,128,1024]{2,0,1:T(4,128)(2,1)S(1)} %bitcast.526), kind=kLoop, calls=%fused_computation.6 | loop fusion | flops 8912896 | bytes 4456448 | tf_op jit(solution)/shard_map/concatenate | solution.py:56
  13.2 73.1 %all_to_all.16 = bf16[128,4,1,2176]{3,1,2,0:T(4,128)(2,1)S(1)} all-to-all(bf16[128,4,1,2176]{3,1,2,0:T(4,128)(2,1)S(1)} %constant_dynamic-update-slice_fusion), channel_id=1, replica_groups=mesh['row'=16,'col'=8,'rep'=4] {'row','col'}, dimensions={0} | all-to-all | bytes 4456448 | tf_op jit(solution)/shard_map/all_to_all | solution.py:61
  86.2 1.8 %convert_reduce_fusion.1 = (f32[2176]{0:T(1024)S(1)}, f32[2176]{0:T(1024)S(1)}) fusion(bf16[128,4,1,2176]{3,1,2,0:T(4,128)(2,1)S(1)} %all_to_all.16), kind=kLoop, calls=%fused_computation.7 | loop fusion | flops 4452096 | bytes 2245632 | tf_op jit(solution)/shard_map/reduce_sum | solution.py:66
  88.0 0.7 broadcast_in_dim.26
  88.7 4.0 %all-to-all-start.1 = ((f32[4,1,4352]{2,1,0:T(1,128)}), f32[4,1,4352]{2,1,0:T(1,128)S(1)}, u32[]{:S(2)}, u32[]{:S(2)}) async-start(f32[4,1,4352]{2,1,0:T(1,128)} %broadcast_in_dim.26), calls=%async_computation.1 | async-start | bytes 139264 | tf_op jit(solution)/shard_map/all_to_all | solution.py:10
  92.7 2.6 %reshape.42 = f32[512,2176]{1,0:T(8,128)} reshape(bf16[128,4,1,2176]{3,1,2,0:T(4,128)(2,1)S(1)} %all_to_all.16) | data formatting | bytes 6684672 | tf_op jit(solution)/shard_map/convert_element_type | solution.py:64
  95.3 1.9 %all-to-all-done.1 = f32[4,1,4352]{2,1,0:T(1,128)S(1)} async-done(((f32[4,1,4352]{2,1,0:T(1,128)}), f32[4,1,4352]{2,1,0:T(1,128)S(1)}, u32[]{:S(2)}, u32[]{:S(2)}) %all-to-all-start.1) | async-done | bytes 69664 | tf_op jit(solution)/shard_map/all_to_all | solution.py:10
  97.2 0.1 reduce_sum.38
  97.3 2.7 %multiply_convert_fusion = bf16[512,2176]{1,0:T(8,128)(2,1)S(1)} fusion(f32[512,2176]{1,0:T(8,128)} %reshape.42, f32[2176]{0:T(1024)S(1)} %get-tuple-element.7, f32[2176]{0:T(1024)S(1)} %get-tuple-element.6), kind=kLoop, calls=%fused_computation.3 | loop fusion | flops 3342336 | bytes 6702080 | tf_op jit(solution)/shard_map/convert_element_type | solution.py:70
  100.0 0.1 slice.45
  100.1 1.6 %fusion = bf16[1024,1152]{1,0:T(8,128)(2,1)S(1)} fusion(bf16[512,128]{1,0:T(8,128)(2,1)S(1)} %slice.46, bf16[512,1024]{1,0:T(8,128)(2,1)S(1)} %slice.45, bf16[512,2176]{1,0:T(8,128)(2,1)S(1)} %multiply_convert_fusion), kind=kOutput, calls=%fused_computation.5 | convolution fusion | flops 1212678144 | bytes 4587520 | tf_op jit(solution)/shard_map/dot_general | solution.py:75
  101.7 31.5 %all_to_all.17 = bf16[4,256,1152]{2,1,0:T(8,128)(2,1)S(1)} all-to-all(bf16[4,256,1152]{2,1,0:T(8,128)(2,1)S(1)} %bitcast.528), channel_id=1, replica_groups=mesh['row'=16,'col'=8,'rep'=4] {'rep'}, dimensions={0} | all-to-all | bytes 4718592 | tf_op jit(solution)/shard_map/all_to_all | solution.py:32
  133.2 0.3 convert_reduce_fusion
  133.5 0.7 slice_bitcast_fusion.1
  134.2 1.1 slice_bitcast_fusion
  (131 shorter events, 2.2 us)
Async XLA Ops:
  0.6 4.0 %copy-start = (bf16[4,16384]{1,0:T(4,128)(2,1)S(1)}, bf16[4,16384]{1,0:T(4,128)(2,1)}, u32[]{:S(2)}) copy-start(bf16[4,16384]{1,0:T(4,128)(2,1)} %param.2) | copy-start | bytes 393220
  88.7 8.5 %all-to-all-start.1 = ((f32[4,1,4352]{2,1,0:T(1,128)}), f32[4,1,4352]{2,1,0:T(1,128)S(1)}, u32[]{:S(2)}, u32[]{:S(2)}) async-start(f32[4,1,4352]{2,1,0:T(1,128)} %broadcast_in_dim.26), calls=%async_computation.1 | async-start | bytes 139264 | tf_op jit(solution)/shard_map/all_to_all | solution.py:10
